TPU v7x, 32 devices: a whole 2x2x4 slice. The times are simulated.
32 devices in a mesh: grp: 2 (over x), slab: 16 (over z, y, core).
Axes of the slice: x: 2, y: 2, z: 4, core: 2. Of those that a mesh axis runs over, the one named last changes fastest.
Arguments:
- image: float32 [2, 384, 192, 256], P(None, ('grp', 'slab')), parts along dimension 1, may hold values from -6 to 6
- adjoint_data: bfloat16 [2, 384, 192, 256], P(None, ('grp', 'slab')), parts along dimension 1, may hold values from -6 to 6
- coil_maps: bfloat16 [8, 2, 384, 192, 256], P(None, None, ('grp', 'slab')), parts along dimension 2, may hold values from -2.5 to 2.5
- masks: int32 [1, 384, 192], P(None, 'grp'), parts along dimension 1, may hold values 0 or 1
- sources: int32 [1, 1152, 2], P(None, ('grp', 'slab')), parts along dimension 1, may hold values from 0 to 575, as said below
- weights: bfloat16 [1, 1152, 8192], P(None, ('grp', 'slab')), parts along dimension 1, may hold values from -0.5 to 0.5
Outputs:
- updated: float32 [2, 384, 192, 256], P(None, ('grp', 'slab')), parts along dimension 1
There are 2 independent parts, one for each index of `grp`. A program takes and returns all parts, laid end to end along the dimension named above; each array names one. Nothing has to cross between parts.
Inputs may be any that keep to these rules, and one draw needn't show every extreme that they name: sources[s, t, j] is a block number (plane * 3 + y block); its plane lies within 24 planes of target block t's plane, and its y block within one of t's y block.
All inputs are finite; a program needn't handle non-finite values.
Results may differ from a plain program's by a relative error of at most 0.005.
Values may be sent and summed in bfloat16 or wider, within the bound.
No kernel may reach another device: no remote copies, remote signals or barrier semaphores. Data moves between devices by JAX's collectives and lax.ppermute only.
A program may use at most 256 MiB of HBM per device.

v0:
```python
import math
import jax
import jax.numpy as jnp
from jax import lax
from jax.sharding import PartitionSpec as P

NX = 192
NY = 192
NZ = 256
BLK = 64
REACH = 2


def shifted(shard, axis, by):
    count = lax.axis_size(axis)
    pairs = [(i, i + by) for i in range(count) if 0 <= i + by < count]
    return lax.ppermute(shard, axis, pairs)


def dft_table(length, direction):
    positions = jnp.arange(length, dtype=jnp.int32)
    product = positions[:, None] * positions[None, :] % length
    phases = product.astype(jnp.float32) * (2.0 * math.pi / length)
    factor = 1.0 / math.sqrt(length)
    cosine = jnp.cos(phases) * factor
    sine_part = jnp.sin(phases) * (direction * factor)
    upper_rows = jnp.stack([cosine, -sine_part], axis=1)
    lower_rows = jnp.stack([sine_part, cosine], axis=1)
    return jnp.stack([upper_rows, lower_rows], axis=0).astype(jnp.bfloat16)


def column_y(volume, matrix):
    return jnp.einsum("zcpxj,qkpj->zcqxk", volume, matrix, preferred_element_type=jnp.float32)


def column_x(volume, matrix):
    return jnp.einsum("zcpjy,qkpj->zcqky", volume, matrix, preferred_element_type=jnp.float32)


def expand_columns(sensitivity, warped):
    real_map = sensitivity[:, :, 0].astype(jnp.float32)
    imag_map = sensitivity[:, :, 1].astype(jnp.float32)
    real_warp = warped[:, 0][:, None]
    imag_warp = warped[:, 1][:, None]
    real_part = real_map * real_warp - imag_map * imag_warp
    imag_part = real_map * imag_warp + imag_map * real_warp
    return jnp.stack([real_part, imag_part], axis=2).astype(jnp.bfloat16)


def combine_columns(sensitivity, returned):
    real_map = sensitivity[:, :, 0].astype(jnp.float32)
    imag_map = sensitivity[:, :, 1].astype(jnp.float32)
    real_part = jnp.sum(real_map * returned[:, :, 0] + imag_map * returned[:, :, 1], axis=1)
    imag_part = jnp.sum(real_map * returned[:, :, 1] - imag_map * returned[:, :, 0], axis=1)
    return jnp.stack([real_part, imag_part], axis=1)


def per_device(image, adjoint_data, coil_maps, masks, sources, weights):
    slab_rank = lax.axis_index("slab")
    planes = image.shape[1]
    y_blocks = NY // BLK
    local_blocks = planes * y_blocks
    reach_slots = 2 * REACH + 1
    rounded = image.astype(jnp.bfloat16)
    forward_y = dft_table(NY, -1.0)
    inverse_y = dft_table(NY, 1.0)
    forward_x = dft_table(NX, -1.0)
    inverse_x = dft_table(NX, 1.0)
    nearby_list = []
    for offset in range(-REACH, REACH + 1):
        if offset == 0:
            nearby_list.append(rounded)
        else:
            nearby_list.append(shifted(rounded, "slab", -offset))
    nearby = jnp.stack(nearby_list, axis=1).reshape(2, reach_slots * local_blocks, BLK, NZ)
    maps_leading = jnp.transpose(coil_maps, (4, 0, 1, 2, 3))
    maps_columns = lax.all_to_all(maps_leading, "slab", split_axis=0, concat_axis=3, tiled=True)
    gradient = jnp.zeros((2, local_blocks, BLK, NZ), jnp.float32)
    link_ids = sources[0]
    matrices = weights[0].reshape(local_blocks, 2, BLK, BLK)
    positions = link_ids - (slab_rank - REACH) * local_blocks
    warped = jnp.zeros((2, local_blocks, BLK, NZ), jnp.float32)
    for member in range(2):
        picked = jnp.take(nearby, positions[:, member], axis=1)
        warped = warped + jnp.einsum(
            "tij,rtjz->rtiz", matrices[:, member], picked, preferred_element_type=jnp.float32
        )
    warped = warped.reshape(2, planes, NY, NZ)
    sampled = masks[0].astype(jnp.float32)
    warped_leading = jnp.transpose(warped, (3, 0, 1, 2))
    warped_columns = lax.all_to_all(warped_leading, "slab", split_axis=0, concat_axis=2, tiled=True)
    spectra = column_y(expand_columns(maps_columns, warped_columns), forward_y).astype(jnp.bfloat16)
    middle = (column_x(spectra, forward_x) * sampled[None, None, None, :, :]).astype(jnp.bfloat16)
    restored = column_x(middle, inverse_x).astype(jnp.bfloat16)
    combined_columns = combine_columns(maps_columns, column_y(restored, inverse_y)).astype(
        jnp.bfloat16
    )
    back_leading = lax.all_to_all(combined_columns, "slab", split_axis=2, concat_axis=0, tiled=True)
    grad_image = jnp.transpose(back_leading, (1, 2, 3, 0))
    grad_blocks = grad_image.reshape(2, local_blocks, BLK, NZ)
    spread = jnp.zeros((2, reach_slots * local_blocks, BLK, NZ), jnp.float32)
    for member in range(2):
        product = jnp.einsum(
            "tij,rtiz->rtjz", matrices[:, member], grad_blocks, preferred_element_type=jnp.float32
        )
        spread = spread.at[:, positions[:, member]].add(product)
    spread = spread.reshape(2, reach_slots, local_blocks, BLK, NZ)
    for offset in range(-REACH, REACH + 1):
        portion = spread[:, offset + REACH]
        if offset == 0:
            gradient = gradient + portion
        else:
            gradient = gradient + shifted(portion, "slab", offset)
    gradient = gradient.reshape(2, planes, NY, NZ)
    return image - 0.5 * (gradient - adjoint_data.astype(jnp.float32))


def solution(mesh):
    return jax.shard_map(
        per_device,
        mesh=mesh,
        in_specs=(
            P(None, ("grp", "slab"), None, None),
            P(None, ("grp", "slab"), None, None),
            P(None, None, ("grp", "slab"), None, None),
            P(None, "grp", None),
            P(None, ("grp", "slab"), None),
            P(None, ("grp", "slab"), None),
        ),
        out_specs=P(None, ("grp", "slab"), None, None),
        check_vma=False,
    )
```

profile of v0, /device:TPU:9, one launch (start us, length us, event | category | flops | bytes accessed | tf_op | source)
XLA Modules:
  0.0 1518.6 jit_solution(13383456892984787065)
XLA Ops:
  17.7 113.8 %collective-permute-done = bf16[2,12,192,256]{3,2,1,0:T(8,128)(2,1)} collective-permute-done((bf16[2,12,192,256]{3,2,1,0:T(8,128)(2,1)S(1)}, bf16[2,12,192,256]{3,2,1,0:T(8,128)(2,1)}, u32[]{:S(2)}, u32[]{:S(2)}) %collective-permute-start) | collective-permute-done | bytes 2359328 | tf_op jit(solution)/shard_map/ppermute | solution.py:17
  134.9 23.1 %collective-permute-done.1 = bf16[2,12,192,256]{3,2,1,0:T(8,128)(2,1)} collective-permute-done((bf16[2,12,192,256]{3,2,1,0:T(8,128)(2,1)S(1)}, bf16[2,12,192,256]{3,2,1,0:T(8,128)(2,1)}, u32[]{:S(2)}, u32[]{:S(2)}) %collective-permute-start.1) | collective-permute-done | bytes 2359328 | tf_op jit(solution)/shard_map/ppermute | solution.py:17
  187.7 10.1 copy.78
  204.1 34.1 %copy.68 = bf16[8,2,12,192,256]{3,0,2,1,4:T(8,128)(2,1)} copy(bf16[8,2,12,192,256]{4,3,2,1,0:T(8,128)(2,1)} %param.10) | data formatting | bytes 37748736 | tf_op args[2]
  238.2 101.2 %all-to-all-done.1 = f32[256,2,12,192]{3,1,2,0:T(2,128)} async-done(((f32[256,2,12,192]{3,1,2,0:T(2,128)}), f32[256,2,12,192]{3,1,2,0:T(2,128)}, u32[]{:S(2)}, u32[]{:S(2)}) %all-to-all-start.1) | async-done | bytes 4718624 | tf_op jit(solution)/shard_map/all_to_all | solution.py:91
  339.4 7.9 all-to-all-start
  363.0 523.8 %all-to-all-done = bf16[256,8,2,12,192]{4,1,3,2,0:T(8,128)(2,1)} async-done(((bf16[256,8,2,12,192]{4,1,3,2,0:T(8,128)(2,1)}), bf16[256,8,2,12,192]{4,1,3,2,0:T(8,128)(2,1)}, u32[]{:S(2)}, u32[]{:S(2)}) %all-to-all-start) | async-done | bytes 18874400 | tf_op jit(solution)/shard_map/all_to_all | solution.py:77
  886.8 21.2 %copy.69 = bf16[16,8,2,16,12,192]{5,1,4,3,2,0:T(8,128)(2,1)} copy(bf16[16,8,2,16,12,192]{5,1,4,2,0,3:T(8,128)(2,1)} %bitcast.4) | data formatting | bytes 37748736 | tf_op jit(solution)/shard_map/all_to_all | solution.py:77
  908.0 9.8 fusion.77
  917.8 15.8 %fusion.2 = (bf16[16,8,1,192,192]{4,3,2,1,0:T(8,128)(2,1)}, bf16[16,8,1,192,192]{4,3,2,1,0:T(8,128)(2,1)}) fusion(f32[16,192,192]{2,1,0:T(8,128)S(1)} %copy-done.2, f32[16,192,192]{2,1,0:T(8,128)S(1)} %copy.81, bf16[16,8,1,192,192]{4,1,3,2,0:T(8,128)(2,1)S(1)} %get-tuple-element.15, bf16[16,8,1,192,192]{4,1,3,2,0:T(8,128)(2,1)S(1)} %get-tuple-element.14), kind=kLoop, calls=%fused_computation.17 | loop fusion | flops 47185920 | bytes 42467328 | tf_op jit(solution)/shard_map/convert.4
  933.6 22.6 %fusion.16 = bf16[2,192,16,8,192,1]{4,1,5,3,2,0:T(8,128)(2,1)} fusion(bf16[16,8,1,192,192]{4,3,2,1,0:T(8,128)(2,1)} %get-tuple-element.13, bf16[16,8,1,192,192]{4,3,2,1,0:T(8,128)(2,1)} %get-tuple-element.12, bf16[1,192,2,192]{3,1,2,0:T(8,128)(2,1)S(1)} %get-tuple-element.23, bf16[1,192,2,192]{3,1,2,0:T(8,128)(2,1)S(1)} %get-tuple-element.24), kind=kOutput, calls=%fused_computation.30 | convolution fusion | flops 7286095872 | bytes 38043648 | tf_op jit(solution)/shard_map/zcpxj,qkpj->zcqxk/dot_general | solution.py:33
  956.3 22.4 %fusion.15 = bf16[16,8,2,192,192,1]{4,3,1,0,2,5:T(8,128)(2,1)} fusion(f32[192,192]{1,0:T(8,128)S(1)} %copy-done.11, bf16[2,192,16,8,192,1]{4,1,5,3,2,0:T(8,128)(2,1)} %fusion.16, bf16[1,192,2,192]{3,1,2,0:T(8,128)(2,1)S(1)} %get-tuple-element.23, bf16[1,192,2,192]{3,1,2,0:T(8,128)(2,1)S(1)} %get-tuple-element.24), kind=kOutput, calls=%fused_computation.28 | convolution fusion | flops 7267221504 | bytes 38191104 | tf_op jit(solution)/shard_map/zcpjy,qkpj->zcqky/dot_general | solution.py:37
  978.7 34.7 %fusion.21 = f32[16,8,2,192,192]{4,3,2,1,0:T(8,128)} fusion(bf16[16,8,2,192,192,1]{4,3,1,0,2,5:T(8,128)(2,1)} %fusion.15, bf16[1,192,2,192]{3,1,2,0:T(8,128)(2,1)S(1)} %copy-done.9, bf16[1,192,2,192]{3,1,2,0:T(8,128)(2,1)S(1)} %copy-done.8), kind=kOutput, calls=%fused_computation.35 | convolution fusion | flops 14506131456 | bytes 56918016 | tf_op jit(solution)/shard_map/zcpxj,qkpj->zcqxk/dot_general | solution.py:33
  1013.4 26.0 %fusion.6 = (bf16[16,192,192]{2,1,0:T(8,128)(2,1)S(1)}, bf16[16,192,192]{2,1,0:T(8,128)(2,1)S(1)}) fusion(f32[16,8,2,192,192]{4,3,2,1,0:T(8,128)} %fusion.21, bf16[16,8,1,192,192]{4,1,3,2,0:T(8,128)(2,1)} %copy-done.1, bf16[16,8,1,192,192]{4,1,3,2,0:T(8,128)(2,1)} %copy-done), kind=kLoop, calls=%fused_computation.21 | loop fusion | flops 46006272 | bytes 58982400 | tf_op jit(solution)/shard_map/reduce_sum | solution.py:53
  1049.3 7.2 all-to-all-start.2
  1056.6 67.8 %all-to-all-done.2 = bf16[16,2,192,192]{3,0,1,2:T(8,128)(2,1)S(1)} async-done(((bf16[16,2,192,192]{3,0,1,2:T(8,128)(2,1)}), bf16[16,2,192,192]{3,0,1,2:T(8,128)(2,1)S(1)}, u32[]{:S(2)}, u32[]{:S(2)}) %all-to-all-start.2) | async-done | bytes 2359328 | tf_op jit(solution)/shard_map/all_to_all | solution.py:98
  1135.7 10.8 broadcast_in_dim.8
  1146.6 14.6 scatter_fusion
  1161.2 14.7 scatter_fusion.1
  1175.9 7.7 slice_bitcast_fusion.3
  1197.6 245.1 %collective-permute-done.4 = f32[2,36,64,256]{3,2,1,0:T(8,128)S(1)} collective-permute-done((f32[2,36,64,256]{3,2,1,0:T(8,128)S(1)}, f32[2,36,64,256]{3,2,1,0:T(8,128)S(1)}, u32[]{:S(2)}, u32[]{:S(2)}) %collective-permute-start.4) | collective-permute-done | bytes 4718624 | tf_op jit(solution)/shard_map/ppermute | solution.py:17
  1442.7 50.3 %collective-permute-done.5 = f32[2,36,64,256]{3,2,1,0:T(8,128)S(1)} collective-permute-done((f32[2,36,64,256]{3,2,1,0:T(8,128)S(1)}, f32[2,36,64,256]{3,2,1,0:T(8,128)S(1)}, u32[]{:S(2)}, u32[]{:S(2)}) %collective-permute-start.5) | collective-permute-done | bytes 4718624 | tf_op jit(solution)/shard_map/ppermute | solution.py:17
  1497.3 13.2 fusion.32
  1510.6 7.8 fusion.34
  (82 shorter events, 112.3 us)
Async XLA Ops:
  0.0 17.0 %copy-start.14 = (s32[1,36,2]{1,2,0:T(2,128)S(1)}, s32[1,36,2]{1,2,0:T(2,128)}, u32[]{:S(2)}) copy-start(s32[1,36,2]{1,2,0:T(2,128)} %param.12) | copy-start | bytes 868
  2.7 128.9 %collective-permute-start = (bf16[2,12,192,256]{3,2,1,0:T(8,128)(2,1)S(1)}, bf16[2,12,192,256]{3,2,1,0:T(8,128)(2,1)}, u32[]{:S(2)}, u32[]{:S(2)}) collective-permute-start(bf16[2,12,192,256]{3,2,1,0:T(8,128)(2,1)S(1)} %convert_element_type.99), channel_id=1, source_target_pairs={{0,2},{1,3},{2,4},{3,5},{4,6},{5,7},{6,8},{7,9},{8,10},{9,11},{10,... | collective-permute-start | bytes 7077896 | tf_op jit(solution)/shard_map/ppermute | solution.py:17
  5.8 152.2 %collective-permute-start.1 = (bf16[2,12,192,256]{3,2,1,0:T(8,128)(2,1)S(1)}, bf16[2,12,192,256]{3,2,1,0:T(8,128)(2,1)}, u32[]{:S(2)}, u32[]{:S(2)}) collective-permute-start(bf16[2,12,192,256]{3,2,1,0:T(8,128)(2,1)S(1)} %convert_element_type.99), channel_id=1, source_target_pairs={{0,1},{1,2},{2,3},{3,4},{4,5},{5,6},{6,7},{7,8},{8,9},{9,10},{10,1... | collective-permute-start | bytes 7077896 | tf_op jit(solution)/shard_map/ppermute | solution.py:17
  9.8 153.4 %collective-permute-start.2 = (bf16[2,12,192,256]{3,2,1,0:T(8,128)(2,1)S(1)}, bf16[2,12,192,256]{3,2,1,0:T(8,128)(2,1)}, u32[]{:S(2)}, u32[]{:S(2)}) collective-permute-start(bf16[2,12,192,256]{3,2,1,0:T(8,128)(2,1)S(1)} %convert_element_type.99), channel_id=1, source_target_pairs={{1,0},{2,1},{3,2},{4,3},{5,4},{6,5},{7,6},{8,7},{9,8},{10,9},{11,1... | collective-permute-start | bytes 7077896 | tf_op jit(solution)/shard_map/ppermute | solution.py:17
  11.8 154.8 %collective-permute-start.3 = (bf16[2,12,192,256]{3,2,1,0:T(8,128)(2,1)S(1)}, bf16[2,12,192,256]{3,2,1,0:T(8,128)(2,1)}, u32[]{:S(2)}, u32[]{:S(2)}) collective-permute-start(bf16[2,12,192,256]{3,2,1,0:T(8,128)(2,1)S(1)} %convert_element_type.99), channel_id=1, source_target_pairs={{2,0},{3,1},{4,2},{5,3},{6,4},{7,5},{8,6},{9,7},{10,8},{11,9},{12,... | collective-permute-start | bytes 7077896 | tf_op jit(solution)/shard_map/ppermute | solution.py:17
  17.0 167.0 %copy-start.3 = (bf16[36,2,64,64]{3,2,1,0:T(8,128)(2,1)}, bf16[36,2,64,64]{3,2,1,0:T(8,128)(2,1)S(1)}, u32[]{:S(2)}) copy-start(bf16[36,2,64,64]{3,2,1,0:T(8,128)(2,1)S(1)} %reshape_squeeze.3) | copy-start | bytes 1769476
  17.7 143.6 %slice-start = ((s8[4718592]{0:T(1024)(128)(4,1)}), s8[4194304]{0:T(1024)(128)(4,1)S(1)}, s32[]{:S(2)}) async-start(s8[4718592]{0:T(1024)(128)(4,1)} %bitcast.213), calls=%async_computation.3 | async-start | bytes 8388608
  17.7 143.6 %slice-start.1 = ((s8[4718592]{0:T(1024)(128)(4,1)}), s8[524288]{0:T(1024)(128)(4,1)S(1)}, s32[]{:S(2)}) async-start(s8[4718592]{0:T(1024)(128)(4,1)} %bitcast.213), calls=%async_computation.4 | async-start | bytes 1048576
  197.7 141.6 %all-to-all-start.1 = ((f32[256,2,12,192]{3,1,2,0:T(2,128)}), f32[256,2,12,192]{3,1,2,0:T(2,128)}, u32[]{:S(2)}, u32[]{:S(2)}) async-start(f32[256,2,12,192]{3,1,2,0:T(2,128)} %copy.78), calls=%async_computation.1 | async-start | bytes 12582912 | tf_op jit(solution)/shard_map/all_to_all | solution.py:91
  339.4 11.1 copy-start.10
  339.4 547.4 %all-to-all-start = ((bf16[256,8,2,12,192]{4,1,3,2,0:T(8,128)(2,1)}), bf16[256,8,2,12,192]{4,1,3,2,0:T(8,128)(2,1)}, u32[]{:S(2)}, u32[]{:S(2)}) async-start(bf16[256,8,2,12,192]{4,1,3,2,0:T(8,128)(2,1)} %bitcast.212), calls=%async_computation | async-start | bytes 50331648 | tf_op jit(solution)/shard_map/all_to_all | solution.py:77
  908.0 9.8 copy-start.2
  917.8 15.9 %copy-start = (bf16[16,8,1,192,192]{4,1,3,2,0:T(8,128)(2,1)}, bf16[16,8,1,192,192]{4,1,3,2,0:T(8,128)(2,1)S(1)}, u32[]{:S(2)}) copy-start(bf16[16,8,1,192,192]{4,1,3,2,0:T(8,128)(2,1)S(1)} %get-tuple-element.14) | copy-start | bytes 28311556
  917.8 15.8 %copy-start.1 = (bf16[16,8,1,192,192]{4,1,3,2,0:T(8,128)(2,1)}, bf16[16,8,1,192,192]{4,1,3,2,0:T(8,128)(2,1)S(1)}, u32[]{:S(2)}) copy-start(bf16[16,8,1,192,192]{4,1,3,2,0:T(8,128)(2,1)S(1)} %get-tuple-element.15) | copy-start | bytes 28311556
  933.6 22.6 %copy-start.11 = (f32[192,192]{1,0:T(8,128)S(1)}, f32[192,192]{1,0:T(8,128)}, u32[]{:S(2)}) copy-start(f32[192,192]{1,0:T(8,128)} %convert_bitcast_fusion.2) | copy-start | bytes 442372
  956.3 22.4 %copy-start.8 = (bf16[1,192,2,192]{3,1,2,0:T(8,128)(2,1)S(1)}, bf16[1,192,2,192]{3,1,2,0:T(8,128)(2,1)}, u32[]{:S(2)}) copy-start(bf16[1,192,2,192]{3,1,2,0:T(8,128)(2,1)} %get-tuple-element.22) | copy-start | bytes 442372
  956.3 22.4 %copy-start.9 = (bf16[1,192,2,192]{3,1,2,0:T(8,128)(2,1)S(1)}, bf16[1,192,2,192]{3,1,2,0:T(8,128)(2,1)}, u32[]{:S(2)}) copy-start(bf16[1,192,2,192]{3,1,2,0:T(8,128)(2,1)} %get-tuple-element.25) | copy-start | bytes 442372
  1049.3 7.2 copy-start.13
  1049.3 75.0 %all-to-all-start.2 = ((bf16[16,2,192,192]{3,0,1,2:T(8,128)(2,1)}), bf16[16,2,192,192]{3,0,1,2:T(8,128)(2,1)S(1)}, u32[]{:S(2)}, u32[]{:S(2)}) async-start(bf16[16,2,192,192]{3,0,1,2:T(8,128)(2,1)} %copy.89), calls=%async_computation.2 | async-start | bytes 6291456 | tf_op jit(solution)/shard_map/all_to_all | solution.py:98
  1183.6 259.1 %collective-permute-start.4 = (f32[2,36,64,256]{3,2,1,0:T(8,128)S(1)}, f32[2,36,64,256]{3,2,1,0:T(8,128)S(1)}, u32[]{:S(2)}, u32[]{:S(2)}) collective-permute-start(f32[2,36,64,256]{3,2,1,0:T(8,128)S(1)} %get-tuple-element.17), channel_id=1, source_target_pairs={{2,0},{3,1},{4,2},{5,3},{6,4},{7,5},{8,6},{9,7},{10,8},{11,9},{12,... | collective-permute-start | bytes 14155784 | tf_op jit(solution)/shard_map/ppermute | solution.py:17
  1185.5 307.4 %collective-permute-start.5 = (f32[2,36,64,256]{3,2,1,0:T(8,128)S(1)}, f32[2,36,64,256]{3,2,1,0:T(8,128)S(1)}, u32[]{:S(2)}, u32[]{:S(2)}) collective-permute-start(f32[2,36,64,256]{3,2,1,0:T(8,128)S(1)} %get-tuple-element.16), channel_id=1, source_target_pairs={{1,0},{2,1},{3,2},{4,3},{5,4},{6,5},{7,6},{8,7},{9,8},{10,9},{11,1... | collective-permute-start | bytes 14155784 | tf_op jit(solution)/shard_map/ppermute | solution.py:17
  1188.5 304.5 %collective-permute-start.6 = (f32[2,36,64,256]{3,2,1,0:T(8,128)S(1)}, f32[2,36,64,256]{3,2,1,0:T(8,128)S(1)}, u32[]{:S(2)}, u32[]{:S(2)}) collective-permute-start(f32[2,36,64,256]{3,2,1,0:T(8,128)S(1)} %get-tuple-element.19), channel_id=1, source_target_pairs={{0,1},{1,2},{2,3},{3,4},{4,5},{5,6},{6,7},{7,8},{8,9},{9,10},{10,1... | collective-permute-start | bytes 14155784 | tf_op jit(solution)/shard_map/ppermute | solution.py:17
  1192.2 305.1 %collective-permute-start.7 = (f32[2,36,64,256]{3,2,1,0:T(8,128)S(1)}, f32[2,36,64,256]{3,2,1,0:T(8,128)}, u32[]{:S(2)}, u32[]{:S(2)}) collective-permute-start(f32[2,36,64,256]{3,2,1,0:T(8,128)S(1)} %get-tuple-element.18), channel_id=1, source_target_pairs={{0,2},{1,3},{2,4},{3,5},{4,6},{5,7},{6,8},{7,9},{8,10},{9,11},{10,... | collective-permute-start | bytes 14155784 | tf_op jit(solution)/shard_map/ppermute | solution.py:17
  1442.7 50.3 %copy-start.5 = (f32[2,36,64,256]{3,2,1,0:T(8,128)}, f32[2,36,64,256]{3,2,1,0:T(8,128)S(1)}, u32[]{:S(2)}) copy-start(f32[2,36,64,256]{3,2,1,0:T(8,128)S(1)} %collective-permute-done.4) | copy-start | bytes 14155780
  (4 other events, 8.4 us)
where the time goes:
time: 1530 us; the launch traced here: 1520 us
  waiting for transfers between devices  1130 us (74%)
  local copies, waits for them, and re-layouts  153 us (10%)
  other arithmetic  103 us (7%)
  matrix products  89.1 us (6%)
  starting transfers between devices  47.5 us (3%)
    all_to_all x1, waiting for transfers between devices, per_device(): lax.all_to_all(maps_leading, 'slab', split_axis=0, concat_axis=3, tiled=T...  524 us
    ppermute x8, waiting for transfers between devices, shifted(): return lax.ppermute(shard, axis, pairs)  432 us
    all_to_all x1, waiting for transfers between devices, per_device(): lax.all_to_all(warped_leading, 'slab', split_axis=0, concat_axis=2, tiled...  101 us
    all_to_all x1, waiting for transfers between devices, per_device(): lax.all_to_all(combined_columns, 'slab', split_axis=2, concat_axis=0, til...  67.8 us
    dot_general x2, matrix products, column_y(): jnp.einsum('zcpxj,qkpj->zcqxk', volume, matrix, preferred_element_type=jn...  57.3 us
    unnamed x40, local copies, waits for them, and re-layouts  52.6 us
  transfers between devices with their start and end apart: 11, of which 7 were waited for; matrix products, arithmetic and copies ran while one was open for 4% of the time, Pallas kernels for 0%

commit v1 on v0

--- a/solution.py
+++ b/solution.py
@@ -88,7 +88,12 @@
     warped = warped.reshape(2, planes, NY, NZ)
     sampled = masks[0].astype(jnp.float32)
     warped_leading = jnp.transpose(warped, (3, 0, 1, 2))
-    warped_columns = lax.all_to_all(warped_leading, "slab", split_axis=0, concat_axis=2, tiled=True)
+    warped_columns = jnp.concatenate(
+        lax.all_to_all(
+            jnp.stack(jnp.split(warped_leading, lax.axis_size("slab"), axis=0)), "slab", 0, 0
+        ),
+        axis=2,
+    )
     spectra = column_y(expand_columns(maps_columns, warped_columns), forward_y).astype(jnp.bfloat16)
     middle = (column_x(spectra, forward_x) * sampled[None, None, None, :, :]).astype(jnp.bfloat16)
     restored = column_x(middle, inverse_x).astype(jnp.bfloat16)

time: 1530 us -> 1590 us (1.039)
  local copies, waits for them, and re-layouts: 153 us -> 216 us
    another operation x0 -> x18, local copies, waits for them, and re-layouts: none -> 59.3 us  [per_device(): jnp.stack(jnp.split(warped_leading, lax.axis_size('slab'), axis=0))]
    unnamed x40 -> x75, local copies, waits for them, and re-layouts: 52.6 us -> 70.6 us
where the time goes in v1:
time: 1590 us; the launch traced here: 1580 us
  waiting for transfers between devices  1130 us (71%)
  local copies, waits for them, and re-layouts  216 us (14%)
  other arithmetic  102 us (6%)
  matrix products  89.5 us (6%)
  starting transfers between devices  47.7 us (3%)
    all_to_all x1, waiting for transfers between devices, per_device(): lax.all_to_all(maps_leading, 'slab', split_axis=0, concat_axis=3, tiled=T...  526 us
    ppermute x8, waiting for transfers between devices, shifted(): return lax.ppermute(shard, axis, pairs)  432 us
    all_to_all x1, waiting for transfers between devices, per_device(): lax.all_to_all(jnp.stack(jnp.split(warped_leading, lax.axis_size('slab'),...  101 us
    unnamed x75, local copies, waits for them, and re-layouts  70.6 us
    all_to_all x1, waiting for transfers between devices, per_device(): lax.all_to_all(combined_columns, 'slab', split_axis=2, concat_axis=0, til...  67.8 us
    another operation x18, local copies, waits for them, and re-layouts, per_device(): jnp.stack(jnp.split(warped_leading, lax.axis_size('slab'), axis=0))  59.3 us
    dot_general x2, matrix products, column_y(): jnp.einsum('zcpxj,qkpj->zcqxk', volume, matrix, preferred_element_type=jn...  57.8 us
  transfers between devices with their start and end apart: 11, of which 7 were waited for; matrix products, arithmetic and copies ran while one was open for 4% of the time, Pallas kernels for 0%

profile of v1, /device:TPU:9, one launch (start us, length us, event | category | flops | bytes accessed | tf_op | source)
XLA Modules:
  0.0 1583.5 jit_solution(6379233890252979142)
XLA Ops:
  17.7 113.9 %collective-permute-done = bf16[2,12,192,256]{3,2,1,0:T(8,128)(2,1)} collective-permute-done((bf16[2,12,192,256]{3,2,1,0:T(8,128)(2,1)S(1)}, bf16[2,12,192,256]{3,2,1,0:T(8,128)(2,1)}, u32[]{:S(2)}, u32[]{:S(2)}) %collective-permute-start) | collective-permute-done | bytes 2359328 | tf_op jit(solution)/shard_map/ppermute | solution.py:17
  134.9 23.1 %collective-permute-done.1 = bf16[2,12,192,256]{3,2,1,0:T(8,128)(2,1)} collective-permute-done((bf16[2,12,192,256]{3,2,1,0:T(8,128)(2,1)S(1)}, bf16[2,12,192,256]{3,2,1,0:T(8,128)(2,1)}, u32[]{:S(2)}, u32[]{:S(2)}) %collective-permute-start.1) | collective-permute-done | bytes 2359328 | tf_op jit(solution)/shard_map/ppermute | solution.py:17
  185.4 15.4 slice_bitcast_fusion.7
  269.1 34.1 %copy.49 = bf16[8,2,12,192,256]{3,0,2,1,4:T(8,128)(2,1)} copy(bf16[8,2,12,192,256]{4,3,2,1,0:T(8,128)(2,1)} %param.10) | data formatting | bytes 37748736 | tf_op args[2]
  303.1 101.2 %all-to-all-done.1 = f32[16,16,2,12,192]{4,1,3,2,0:T(8,128)} async-done(((f32[16,16,2,12,192]{4,1,3,2,0:T(8,128)}), f32[16,16,2,12,192]{4,1,3,2,0:T(8,128)}, u32[]{:S(2)}, u32[]{:S(2)}) %all-to-all-start.1) | async-done | bytes 4718624 | tf_op jit(solution)/shard_map/all_to_all | solution.py:92
  404.3 7.5 all-to-all-start
  425.4 526.1 %all-to-all-done = bf16[256,8,2,12,192]{4,1,3,2,0:T(8,128)(2,1)} async-done(((bf16[256,8,2,12,192]{4,1,3,2,0:T(8,128)(2,1)}), bf16[256,8,2,12,192]{4,1,3,2,0:T(8,128)(2,1)}, u32[]{:S(2)}, u32[]{:S(2)}) %all-to-all-start) | async-done | bytes 18874400 | tf_op jit(solution)/shard_map/all_to_all | solution.py:77
  951.4 21.1 %copy.50 = bf16[16,8,2,16,12,192]{5,1,4,3,2,0:T(8,128)(2,1)} copy(bf16[16,8,2,16,12,192]{5,1,4,2,0,3:T(8,128)(2,1)} %bitcast.4) | data formatting | bytes 37748736 | tf_op jit(solution)/shard_map/all_to_all | solution.py:77
  972.6 9.8 fusion.77
  982.4 15.9 %fusion.2 = (bf16[16,8,1,192,192]{4,3,2,1,0:T(8,128)(2,1)}, bf16[16,8,1,192,192]{4,3,2,1,0:T(8,128)(2,1)}) fusion(f32[16,192,192]{2,1,0:T(8,128)S(1)} %copy-done.2, f32[16,192,192]{2,1,0:T(8,128)S(1)} %copy.76, bf16[16,8,1,192,192]{4,1,3,2,0:T(8,128)(2,1)S(1)} %get-tuple-element.15, bf16[16,8,1,192,192]{4,1,3,2,0:T(8,128)(2,1)S(1)} %get-tuple-element.14), kind=kLoop, calls=%fused_computation.17 | loop fusion | flops 47185920 | bytes 42467328 | tf_op jit(solution)/shard_map/convert.4
  998.3 23.0 %fusion.16 = bf16[2,192,16,8,192,1]{4,1,5,3,2,0:T(8,128)(2,1)} fusion(bf16[16,8,1,192,192]{4,3,2,1,0:T(8,128)(2,1)} %get-tuple-element.13, bf16[16,8,1,192,192]{4,3,2,1,0:T(8,128)(2,1)} %get-tuple-element.12, bf16[1,192,2,192]{3,1,2,0:T(8,128)(2,1)S(1)} %get-tuple-element.39, bf16[1,192,2,192]{3,1,2,0:T(8,128)(2,1)S(1)} %get-tuple-element.40), kind=kOutput, calls=%fused_computation.30 | convolution fusion | flops 7286095872 | bytes 38043648 | tf_op jit(solution)/shard_map/zcpxj,qkpj->zcqxk/dot_general | solution.py:33
  1021.3 22.4 %fusion.15 = bf16[16,8,2,192,192,1]{4,3,1,0,2,5:T(8,128)(2,1)} fusion(f32[192,192]{1,0:T(8,128)S(1)} %copy-done.21, bf16[2,192,16,8,192,1]{4,1,5,3,2,0:T(8,128)(2,1)} %fusion.16, bf16[1,192,2,192]{3,1,2,0:T(8,128)(2,1)S(1)} %get-tuple-element.39, bf16[1,192,2,192]{3,1,2,0:T(8,128)(2,1)S(1)} %get-tuple-element.40), kind=kOutput, calls=%fused_computation.28 | convolution fusion | flops 7267221504 | bytes 38191104 | tf_op jit(solution)/shard_map/zcpjy,qkpj->zcqky/dot_general | solution.py:37
  1043.8 34.7 %fusion.21 = f32[16,8,2,192,192]{4,3,2,1,0:T(8,128)} fusion(bf16[16,8,2,192,192,1]{4,3,1,0,2,5:T(8,128)(2,1)} %fusion.15, bf16[1,192,2,192]{3,1,2,0:T(8,128)(2,1)S(1)} %copy-done.19, bf16[1,192,2,192]{3,1,2,0:T(8,128)(2,1)S(1)} %copy-done.18), kind=kOutput, calls=%fused_computation.35 | convolution fusion | flops 14506131456 | bytes 56918016 | tf_op jit(solution)/shard_map/zcpxj,qkpj->zcqxk/dot_general | solution.py:33
  1078.5 25.8 %fusion.6 = (bf16[16,192,192]{2,1,0:T(8,128)(2,1)S(1)}, bf16[16,192,192]{2,1,0:T(8,128)(2,1)S(1)}) fusion(f32[16,8,2,192,192]{4,3,2,1,0:T(8,128)} %fusion.21, bf16[16,8,1,192,192]{4,1,3,2,0:T(8,128)(2,1)} %copy-done.1, bf16[16,8,1,192,192]{4,1,3,2,0:T(8,128)(2,1)} %copy-done), kind=kLoop, calls=%fused_computation.21 | loop fusion | flops 46006272 | bytes 58982400 | tf_op jit(solution)/shard_map/reduce_sum | solution.py:53
  1114.3 7.2 all-to-all-start.2
  1121.5 67.8 %all-to-all-done.2 = bf16[16,2,192,192]{3,0,1,2:T(8,128)(2,1)S(1)} async-done(((bf16[16,2,192,192]{3,0,1,2:T(8,128)(2,1)}), bf16[16,2,192,192]{3,0,1,2:T(8,128)(2,1)S(1)}, u32[]{:S(2)}, u32[]{:S(2)}) %all-to-all-start.2) | async-done | bytes 2359328 | tf_op jit(solution)/shard_map/all_to_all | solution.py:103
  1200.7 10.8 broadcast_in_dim.8
  1211.5 14.3 scatter_fusion
  1225.8 14.3 scatter_fusion.1
  1240.1 7.7 slice_bitcast_fusion.3
  1262.4 245.1 %collective-permute-done.4 = f32[2,36,64,256]{3,2,1,0:T(8,128)S(1)} collective-permute-done((f32[2,36,64,256]{3,2,1,0:T(8,128)S(1)}, f32[2,36,64,256]{3,2,1,0:T(8,128)S(1)}, u32[]{:S(2)}, u32[]{:S(2)}) %collective-permute-start.4) | collective-permute-done | bytes 4718624 | tf_op jit(solution)/shard_map/ppermute | solution.py:17
  1507.5 50.4 %collective-permute-done.5 = f32[2,36,64,256]{3,2,1,0:T(8,128)S(1)} collective-permute-done((f32[2,36,64,256]{3,2,1,0:T(8,128)S(1)}, f32[2,36,64,256]{3,2,1,0:T(8,128)S(1)}, u32[]{:S(2)}, u32[]{:S(2)}) %collective-permute-start.5) | collective-permute-done | bytes 4718624 | tf_op jit(solution)/shard_map/ppermute | solution.py:17
  1562.2 13.2 fusion.32
  1575.5 7.8 fusion.34
  (133 shorter events, 170.2 us)
Async XLA Ops:
  0.0 17.0 %copy-start.24 = (s32[1,36,2]{1,2,0:T(2,128)S(1)}, s32[1,36,2]{1,2,0:T(2,128)}, u32[]{:S(2)}) copy-start(s32[1,36,2]{1,2,0:T(2,128)} %param.12) | copy-start | bytes 868
  2.7 128.9 %collective-permute-start = (bf16[2,12,192,256]{3,2,1,0:T(8,128)(2,1)S(1)}, bf16[2,12,192,256]{3,2,1,0:T(8,128)(2,1)}, u32[]{:S(2)}, u32[]{:S(2)}) collective-permute-start(bf16[2,12,192,256]{3,2,1,0:T(8,128)(2,1)S(1)} %convert_element_type.99), channel_id=1, source_target_pairs={{0,2},{1,3},{2,4},{3,5},{4,6},{5,7},{6,8},{7,9},{8,10},{9,11},{10,... | collective-permute-start | bytes 7077896 | tf_op jit(solution)/shard_map/ppermute | solution.py:17
  5.8 152.2 %collective-permute-start.1 = (bf16[2,12,192,256]{3,2,1,0:T(8,128)(2,1)S(1)}, bf16[2,12,192,256]{3,2,1,0:T(8,128)(2,1)}, u32[]{:S(2)}, u32[]{:S(2)}) collective-permute-start(bf16[2,12,192,256]{3,2,1,0:T(8,128)(2,1)S(1)} %convert_element_type.99), channel_id=1, source_target_pairs={{0,1},{1,2},{2,3},{3,4},{4,5},{5,6},{6,7},{7,8},{8,9},{9,10},{10,1... | collective-permute-start | bytes 7077896 | tf_op jit(solution)/shard_map/ppermute | solution.py:17
  9.8 153.4 %collective-permute-start.2 = (bf16[2,12,192,256]{3,2,1,0:T(8,128)(2,1)S(1)}, bf16[2,12,192,256]{3,2,1,0:T(8,128)(2,1)}, u32[]{:S(2)}, u32[]{:S(2)}) collective-permute-start(bf16[2,12,192,256]{3,2,1,0:T(8,128)(2,1)S(1)} %convert_element_type.99), channel_id=1, source_target_pairs={{1,0},{2,1},{3,2},{4,3},{5,4},{6,5},{7,6},{8,7},{9,8},{10,9},{11,1... | collective-permute-start | bytes 7077896 | tf_op jit(solution)/shard_map/ppermute | solution.py:17
  11.8 154.8 %collective-permute-start.3 = (bf16[2,12,192,256]{3,2,1,0:T(8,128)(2,1)S(1)}, bf16[2,12,192,256]{3,2,1,0:T(8,128)(2,1)}, u32[]{:S(2)}, u32[]{:S(2)}) collective-permute-start(bf16[2,12,192,256]{3,2,1,0:T(8,128)(2,1)S(1)} %convert_element_type.99), channel_id=1, source_target_pairs={{2,0},{3,1},{4,2},{5,3},{6,4},{7,5},{8,6},{9,7},{10,8},{11,9},{12,... | collective-permute-start | bytes 7077896 | tf_op jit(solution)/shard_map/ppermute | solution.py:17
  17.0 167.0 %copy-start.3 = (bf16[36,2,64,64]{3,2,1,0:T(8,128)(2,1)}, bf16[36,2,64,64]{3,2,1,0:T(8,128)(2,1)S(1)}, u32[]{:S(2)}) copy-start(bf16[36,2,64,64]{3,2,1,0:T(8,128)(2,1)S(1)} %reshape_squeeze.3) | copy-start | bytes 1769476
  17.7 143.7 %slice-start = ((s8[4718592]{0:T(1024)(128)(4,1)}), s8[4194304]{0:T(1024)(128)(4,1)S(1)}, s32[]{:S(2)}) async-start(s8[4718592]{0:T(1024)(128)(4,1)} %bitcast.245), calls=%async_computation.3 | async-start | bytes 8388608
  17.7 143.7 %slice-start.1 = ((s8[4718592]{0:T(1024)(128)(4,1)}), s8[524288]{0:T(1024)(128)(4,1)S(1)}, s32[]{:S(2)}) async-start(s8[4718592]{0:T(1024)(128)(4,1)} %bitcast.245), calls=%async_computation.4 | async-start | bytes 1048576
  244.8 13.2 copy-start.14
  244.8 14.0 copy-start.13
  244.8 14.7 copy-start.12
  262.7 141.6 %all-to-all-start.1 = ((f32[16,16,2,12,192]{4,1,3,2,0:T(8,128)}), f32[16,16,2,12,192]{4,1,3,2,0:T(8,128)}, u32[]{:S(2)}, u32[]{:S(2)}) async-start(f32[16,16,2,12,192]{4,1,3,2,0:T(8,128)} %constant_dynamic-update-slice_fusion), calls=%async_computation.1 | async-start | bytes 12582912 | tf_op jit(solution)/shard_map/all_to_all | solution.py:92
  404.3 547.1 %all-to-all-start = ((bf16[256,8,2,12,192]{4,1,3,2,0:T(8,128)(2,1)}), bf16[256,8,2,12,192]{4,1,3,2,0:T(8,128)(2,1)}, u32[]{:S(2)}, u32[]{:S(2)}) async-start(bf16[256,8,2,12,192]{4,1,3,2,0:T(8,128)(2,1)} %bitcast.244), calls=%async_computation | async-start | bytes 50331648 | tf_op jit(solution)/shard_map/all_to_all | solution.py:77
  982.4 15.9 %copy-start = (bf16[16,8,1,192,192]{4,1,3,2,0:T(8,128)(2,1)}, bf16[16,8,1,192,192]{4,1,3,2,0:T(8,128)(2,1)S(1)}, u32[]{:S(2)}) copy-start(bf16[16,8,1,192,192]{4,1,3,2,0:T(8,128)(2,1)S(1)} %get-tuple-element.14) | copy-start | bytes 28311556
  982.4 15.9 %copy-start.1 = (bf16[16,8,1,192,192]{4,1,3,2,0:T(8,128)(2,1)}, bf16[16,8,1,192,192]{4,1,3,2,0:T(8,128)(2,1)S(1)}, u32[]{:S(2)}) copy-start(bf16[16,8,1,192,192]{4,1,3,2,0:T(8,128)(2,1)S(1)} %get-tuple-element.15) | copy-start | bytes 28311556
  998.3 23.0 %copy-start.21 = (f32[192,192]{1,0:T(8,128)S(1)}, f32[192,192]{1,0:T(8,128)}, u32[]{:S(2)}) copy-start(f32[192,192]{1,0:T(8,128)} %convert_bitcast_fusion.2) | copy-start | bytes 442372
  1021.3 22.4 %copy-start.18 = (bf16[1,192,2,192]{3,1,2,0:T(8,128)(2,1)S(1)}, bf16[1,192,2,192]{3,1,2,0:T(8,128)(2,1)}, u32[]{:S(2)}) copy-start(bf16[1,192,2,192]{3,1,2,0:T(8,128)(2,1)} %get-tuple-element.38) | copy-start | bytes 442372
  1021.3 22.4 %copy-start.19 = (bf16[1,192,2,192]{3,1,2,0:T(8,128)(2,1)S(1)}, bf16[1,192,2,192]{3,1,2,0:T(8,128)(2,1)}, u32[]{:S(2)}) copy-start(bf16[1,192,2,192]{3,1,2,0:T(8,128)(2,1)} %get-tuple-element.41) | copy-start | bytes 442372
  1114.3 75.0 %all-to-all-start.2 = ((bf16[16,2,192,192]{3,0,1,2:T(8,128)(2,1)}), bf16[16,2,192,192]{3,0,1,2:T(8,128)(2,1)S(1)}, u32[]{:S(2)}, u32[]{:S(2)}) async-start(bf16[16,2,192,192]{3,0,1,2:T(8,128)(2,1)} %copy.84), calls=%async_computation.2 | async-start | bytes 6291456 | tf_op jit(solution)/shard_map/all_to_all | solution.py:103
  1247.8 259.7 %collective-permute-start.4 = (f32[2,36,64,256]{3,2,1,0:T(8,128)S(1)}, f32[2,36,64,256]{3,2,1,0:T(8,128)S(1)}, u32[]{:S(2)}, u32[]{:S(2)}) collective-permute-start(f32[2,36,64,256]{3,2,1,0:T(8,128)S(1)} %get-tuple-element.17), channel_id=1, source_target_pairs={{2,0},{3,1},{4,2},{5,3},{6,4},{7,5},{8,6},{9,7},{10,8},{11,9},{12,... | collective-permute-start | bytes 14155784 | tf_op jit(solution)/shard_map/ppermute | solution.py:17
  1249.7 308.1 %collective-permute-start.5 = (f32[2,36,64,256]{3,2,1,0:T(8,128)S(1)}, f32[2,36,64,256]{3,2,1,0:T(8,128)S(1)}, u32[]{:S(2)}, u32[]{:S(2)}) collective-permute-start(f32[2,36,64,256]{3,2,1,0:T(8,128)S(1)} %get-tuple-element.16), channel_id=1, source_target_pairs={{1,0},{2,1},{3,2},{4,3},{5,4},{6,5},{7,6},{8,7},{9,8},{10,9},{11,1... | collective-permute-start | bytes 14155784 | tf_op jit(solution)/shard_map/ppermute | solution.py:17
  1252.4 305.4 %collective-permute-start.6 = (f32[2,36,64,256]{3,2,1,0:T(8,128)S(1)}, f32[2,36,64,256]{3,2,1,0:T(8,128)S(1)}, u32[]{:S(2)}, u32[]{:S(2)}) collective-permute-start(f32[2,36,64,256]{3,2,1,0:T(8,128)S(1)} %get-tuple-element.19), channel_id=1, source_target_pairs={{0,1},{1,2},{2,3},{3,4},{4,5},{5,6},{6,7},{7,8},{8,9},{9,10},{10,1... | collective-permute-start | bytes 14155784 | tf_op jit(solution)/shard_map/ppermute | solution.py:17
  1257.1 305.1 %collective-permute-start.7 = (f32[2,36,64,256]{3,2,1,0:T(8,128)S(1)}, f32[2,36,64,256]{3,2,1,0:T(8,128)}, u32[]{:S(2)}, u32[]{:S(2)}) collective-permute-start(f32[2,36,64,256]{3,2,1,0:T(8,128)S(1)} %get-tuple-element.18), channel_id=1, source_target_pairs={{0,2},{1,3},{2,4},{3,5},{4,6},{5,7},{6,8},{7,9},{8,10},{9,11},{10,... | collective-permute-start | bytes 14155784 | tf_op jit(solution)/shard_map/ppermute | solution.py:17
  1507.5 50.4 %copy-start.9 = (f32[2,36,64,256]{3,2,1,0:T(8,128)}, f32[2,36,64,256]{3,2,1,0:T(8,128)S(1)}, u32[]{:S(2)}) copy-start(f32[2,36,64,256]{3,2,1,0:T(8,128)S(1)} %collective-permute-done.4) | copy-start | bytes 14155780
  (14 other events, 109.4 us)
